TPU v7x, 256 devices: a whole 4x4x8 slice. The times are simulated.
256 devices in a mesh: seq: 8 (over z), head: 32 (over y, x, core).
Axes of the slice: x: 4, y: 4, z: 8, core: 2. Of those that a mesh axis runs over, the one named last changes fastest.
Arguments:
- queries: bfloat16 [4096, 32, 128], P(('seq', 'head')), may hold values from -6 to 6
- keys: bfloat16 [4096, 32, 128], P(('seq', 'head')), may hold values from -6 to 6
- values: bfloat16 [4096, 32, 128], P(('seq', 'head')), may hold values from -6 to 6
- out_grad: bfloat16 [4096, 32, 128], P(('seq', 'head')), may hold values from -1.5 to 1.5
- level_weights: float32 [32, 13, 4096], P('head', None, 'seq'), may hold values from 0.2 to 2
Outputs:
- query_grad: bfloat16 [4096, 32, 128], P(('seq', 'head'))
- key_grad: bfloat16 [4096, 32, 128], P(('seq', 'head'))
- value_grad: bfloat16 [4096, 32, 128], P(('seq', 'head'))
- weight_grad: float32 [32, 13, 4096], P('head', None, 'seq')
All inputs are finite; a program needn't handle non-finite values.
Results may differ from a plain program's by a relative error of at most 0.0052.
Values may be sent and summed in bfloat16 or wider, within the bound.
No kernel may reach another device: no remote copies, remote signals or barrier semaphores. Data moves between devices by JAX's collectives and lax.ppermute only.
A program may use at most 64 MiB of HBM per device.

v0:
```python
import math
import jax
import jax.numpy as jnp
from jax import lax
from jax.sharding import PartitionSpec as P


def partner(value, axis, apart):
    mask = 2**apart
    pairs = [(source, source ^ mask) for source in range(lax.axis_size(axis))]
    return lax.ppermute(value, axis, pairs)


def bit_length(values, number):
    running = jnp.zeros(values.shape, jnp.int32)
    for exponent in range(number):
        running = running + (values >= 2**exponent).astype(jnp.int32)
    return running


def level_factor(degree, head_width):
    base_scale = 1.0 / math.sqrt(head_width)
    if degree == 0:
        return base_scale
    return base_scale * 2.0 ** (-(degree - 1) / 2.0)


def spread_states(lower_source, upper_source):
    far_count = lax.axis_size("seq").bit_length() - 1
    position = lax.axis_index("seq")
    lower_states = []
    upper_states = []
    offset = 1
    running = lower_source
    pending = list(upper_source)
    for degree in range(far_count):
        outgoing = [running] + pending[degree:]
        received = partner(jnp.stack(outgoing), "seq", degree)
        upper_bit = position // 2**degree % 2 == 1
        lower_states.append(jnp.where(upper_bit, received[0], 0.0))
        running = running + received[0]
        upper_states.append(jnp.where(upper_bit, 0.0, received[offset]))
        for later_level in range(degree + 1, far_count):
            pending[later_level] = pending[later_level] + received[offset + later_level - degree]
    return (lower_states, upper_states)


def query_states(query_rows, grad_rows, level_weights, first_far):
    head_width = query_rows.shape[2]
    far_count = level_weights.shape[1] - first_far
    coefficients = jnp.stack(
        [
            level_factor(first_far + degree, head_width) * level_weights[:, first_far + degree, :]
            for degree in range(far_count)
        ]
    )
    scaled = (jnp.transpose(coefficients, (0, 2, 1))[..., None] * grad_rows[None]).astype(
        jnp.bfloat16
    )
    states = jnp.einsum("thd,jthe->jhde", query_rows, scaled, preferred_element_type=jnp.float32)
    return (coefficients, [states[degree] for degree in range(far_count)])


def near_terms(query_rows, key_rows, value_rows, grad_rows, level_weights):
    tok_count = query_rows.shape[0]
    heads_here = query_rows.shape[1]
    head_width = query_rows.shape[2]
    block_rows = min(512, tok_count)
    block_bits = block_rows.bit_length() - 1
    local_bits = tok_count.bit_length() - 1
    pieces = tok_count // block_rows
    zero_block = jnp.zeros((block_rows, heads_here, head_width), jnp.float32)
    zero_weights = jnp.zeros((heads_here, block_rows), jnp.float32)
    query_parts = [zero_block] * pieces
    key_parts = [zero_block] * pieces
    value_parts = [zero_block] * pieces
    weight_rows = [[zero_weights] * pieces for degree in range(local_bits + 1)]
    positions = jnp.arange(block_rows, dtype=jnp.int32)
    crossed = jnp.bitwise_xor(positions[:, None], positions[None, :])
    causal = positions[None, :] <= positions[:, None]
    inside = bit_length(crossed, block_bits)
    scores = jnp.einsum("thd,shd->hts", query_rows, key_rows, preferred_element_type=jnp.float32)
    pulls = jnp.einsum("the,she->hts", grad_rows, value_rows, preferred_element_type=jnp.float32)
    product = jnp.where(causal[None], scores * pulls, 0.0)
    weights = jnp.zeros(scores.shape, jnp.float32)
    for degree in range(block_bits + 1):
        factor = level_factor(degree, head_width)
        matching = (causal & (inside == degree))[None]
        column = (factor * level_weights[:, degree, :])[:, :, None]
        weights = jnp.where(matching, column, weights)
        chosen = jnp.sum(jnp.where(matching, product, 0.0), axis=2)
        weight_rows[degree][0] = factor * chosen
    near_scaled = (weights * scores).astype(jnp.bfloat16)
    near_pulled = (weights * pulls).astype(jnp.bfloat16)
    value_parts[0] = jnp.einsum(
        "hts,the->she", near_scaled, grad_rows, preferred_element_type=jnp.float32
    )
    query_parts[0] = jnp.einsum(
        "hts,shd->thd", near_pulled, key_rows, preferred_element_type=jnp.float32
    )
    key_parts[0] = jnp.einsum(
        "hts,thd->shd", near_pulled, query_rows, preferred_element_type=jnp.float32
    )
    weight_near = [jnp.concatenate(weight_rows[degree], axis=1) for degree in range(local_bits + 1)]
    return (query_parts[0], key_parts[0], value_parts[0], weight_near)


def on_device(queries, keys, values, out_grad, level_weights):
    query_rows, key_rows, value_rows, grad_rows = (
        lax.all_to_all(queries, "head", split_axis=1, concat_axis=0, tiled=True),
        lax.all_to_all(keys, "head", split_axis=1, concat_axis=0, tiled=True),
        lax.all_to_all(values, "head", split_axis=1, concat_axis=0, tiled=True),
        lax.all_to_all(out_grad, "head", split_axis=1, concat_axis=0, tiled=True),
    )
    first_far = query_rows.shape[0].bit_length()
    key_state = jnp.einsum("shd,she->hde", key_rows, value_rows, preferred_element_type=jnp.float32)
    coefficients, upper_parts = query_states(query_rows, grad_rows, level_weights, first_far)
    lower_states, upper_states = spread_states(key_state, upper_parts)
    head_width = query_rows.shape[2]
    far_count = level_weights.shape[1] - first_far
    query_near, key_near, value_near, weight_near = near_terms(
        query_rows, key_rows, value_rows, grad_rows, level_weights
    )
    lower_narrow = jnp.stack([matrix.astype(jnp.bfloat16) for matrix in lower_states])
    far_update = jnp.einsum(
        "the,jhde->jthd", grad_rows, lower_narrow, preferred_element_type=jnp.float32
    )
    query_total = query_near + jnp.sum(
        jnp.transpose(coefficients, (0, 2, 1))[..., None] * far_update, axis=0
    )
    upper_total = upper_states[0]
    for degree in range(1, far_count):
        upper_total = upper_total + upper_states[degree]
    upper_narrow = upper_total.astype(jnp.bfloat16)
    key_total = key_near + jnp.einsum(
        "she,hde->shd", value_rows, upper_narrow, preferred_element_type=jnp.float32
    )
    value_total = value_near + jnp.einsum(
        "shd,hde->she", key_rows, upper_narrow, preferred_element_type=jnp.float32
    )
    factors = jnp.array(
        [level_factor(first_far + degree, head_width) for degree in range(far_count)], jnp.float32
    )
    weight_far = factors[:, None, None] * jnp.sum(query_rows[None] * far_update, axis=-1)
    weight_grad = jnp.stack(
        weight_near + [weight_far[degree].T for degree in range(far_count)], axis=1
    )
    query_out, key_out, value_out = (
        lax.all_to_all(
            query_total.astype(jnp.bfloat16), "head", split_axis=0, concat_axis=1, tiled=True
        ),
        lax.all_to_all(
            key_total.astype(jnp.bfloat16), "head", split_axis=0, concat_axis=1, tiled=True
        ),
        lax.all_to_all(
            value_total.astype(jnp.bfloat16), "head", split_axis=0, concat_axis=1, tiled=True
        ),
    )
    return (query_out, key_out, value_out, weight_grad)


def solution(mesh):
    in_specs = (
        P(("seq", "head"), None, None),
        P(("seq", "head"), None, None),
        P(("seq", "head"), None, None),
        P(("seq", "head"), None, None),
        P("head", None, "seq"),
    )
    out_specs = (
        P(("seq", "head"), None, None),
        P(("seq", "head"), None, None),
        P(("seq", "head"), None, None),
        P("head", None, "seq"),
    )
    return jax.shard_map(
        on_device, mesh=mesh, in_specs=in_specs, out_specs=out_specs, check_vma=False
    )
```

profile of v0, /device:TPU:1, one launch (start us, length us, event | category | flops | bytes accessed | tf_op | source)
XLA Modules:
  0.0 130.0 jit_solution(8321953172399653575)
XLA Ops:
  0.6 1.6 %copy.54 = bf16[16,32,128]{2,0,1:T(8,128)(2,1)} copy(bf16[16,32,128]{2,1,0:T(8,128)(2,1)} %param.9) | data formatting | bytes 262144 | tf_op args[3]
  2.2 8.7 %all-to-all-start = ((bf16[16,32,128]{2,0,1:T(8,128)(2,1)}), bf16[16,32,128]{2,0,1:T(8,128)(2,1)S(1)}, u32[]{:S(2)}, u32[]{:S(2)}) async-start(bf16[16,32,128]{2,0,1:T(8,128)(2,1)} %copy.54), calls=%async_computation | async-start | bytes 262144 | tf_op jit(solution)/shard_map/all_to_all | solution.py:113
  11.7 6.9 %all-to-all-done = bf16[16,32,128]{2,0,1:T(8,128)(2,1)S(1)} async-done(((bf16[16,32,128]{2,0,1:T(8,128)(2,1)}), bf16[16,32,128]{2,0,1:T(8,128)(2,1)S(1)}, u32[]{:S(2)}, u32[]{:S(2)}) %all-to-all-start) | async-done | bytes 131104 | tf_op jit(solution)/shard_map/all_to_all | solution.py:113
  18.6 3.9 %all-to-all-start.1 = ((bf16[16,32,128]{2,0,1:T(8,128)(2,1)}), bf16[16,32,128]{2,0,1:T(8,128)(2,1)S(1)}, u32[]{:S(2)}, u32[]{:S(2)}) async-start(bf16[16,32,128]{2,0,1:T(8,128)(2,1)} %copy.55), calls=%async_computation.1 | async-start | bytes 262144 | tf_op jit(solution)/shard_map/all_to_all | solution.py:112
  23.2 7.0 %all-to-all-done.1 = bf16[16,32,128]{2,0,1:T(8,128)(2,1)S(1)} async-done(((bf16[16,32,128]{2,0,1:T(8,128)(2,1)}), bf16[16,32,128]{2,0,1:T(8,128)(2,1)S(1)}, u32[]{:S(2)}, u32[]{:S(2)}) %all-to-all-start.1) | async-done | bytes 131104 | tf_op jit(solution)/shard_map/all_to_all | solution.py:112
  30.2 3.9 %all-to-all-start.2 = ((bf16[16,32,128]{2,0,1:T(8,128)(2,1)}), bf16[16,32,128]{2,0,1:T(8,128)(2,1)S(1)}, u32[]{:S(2)}, u32[]{:S(2)}) async-start(bf16[16,32,128]{2,0,1:T(8,128)(2,1)} %copy.58), calls=%async_computation.2 | async-start | bytes 262144 | tf_op jit(solution)/shard_map/all_to_all | solution.py:111
  34.2 0.8 copy-done.2
  35.9 6.0 %all-to-all-done.2 = bf16[16,32,128]{2,0,1:T(8,128)(2,1)S(1)} async-done(((bf16[16,32,128]{2,0,1:T(8,128)(2,1)}), bf16[16,32,128]{2,0,1:T(8,128)(2,1)S(1)}, u32[]{:S(2)}, u32[]{:S(2)}) %all-to-all-start.2) | async-done | bytes 131104 | tf_op jit(solution)/shard_map/all_to_all | solution.py:111
  41.8 3.9 %all-to-all-start.3 = ((bf16[16,32,128]{2,0,1:T(8,128)(2,1)}), bf16[16,32,128]{2,0,1:T(8,128)(2,1)S(1)}, u32[]{:S(2)}, u32[]{:S(2)}) async-start(bf16[16,32,128]{2,0,1:T(8,128)(2,1)} %copy.62), calls=%async_computation.3 | async-start | bytes 262144 | tf_op jit(solution)/shard_map/all_to_all | solution.py:110
  46.2 7.3 %all-to-all-done.3 = bf16[16,32,128]{2,0,1:T(8,128)(2,1)S(1)} async-done(((bf16[16,32,128]{2,0,1:T(8,128)(2,1)}), bf16[16,32,128]{2,0,1:T(8,128)(2,1)S(1)}, u32[]{:S(2)}, u32[]{:S(2)}) %all-to-all-start.3) | async-done | bytes 131104 | tf_op jit(solution)/shard_map/all_to_all | solution.py:110
  53.5 1.7 %fusion.9 = (f32[512,512]{0,1:T(8,128)S(1)}, bf16[512,512]{0,1:T(8,128)(2,1)S(1)}, f32[512,512]{0,1:T(8,128)}) fusion(f32[512,512]{0,1:T(8,128)S(1)} %fusion.61, f32[512]{0:T(512)S(1)} %bitcast.184, f32[512]{0:T(512)S(1)} %bitcast.186, f32[512]{0:T(512)S(1)} %bitcast.188, f32[512]{0:T(512)S(1)} %bitcast.190, f32[512]{0:T(512)S(1)} %bitcast.192, ...), kind=kOutput, calls=%fused_computation.11 | convolution fusion | flops 83361792 | bytes 3952640 | tf_op jit(solution)/shard_map/thd,shd->hts/dot_general | solution.py:82
  55.2 3.1 %select_reduce_fusion = (f32[512]{0:T(512)S(1)}, f32[512]{0:T(512)S(1)}, f32[512]{0:T(512)S(1)}, f32[512]{0:T(512)S(1)}, f32[512]{0:T(512)S(1)}, /*index=5*/f32[...) fusion(f32[512,512]{0,1:T(8,128)S(1)} %get-tuple-element.28), kind=kLoop, calls=%fused_computation.35 | loop fusion | flops 17820672 | bytes 1069056 | tf_op jit(solution)/shard_map/reduce_sum | solution.py:91
  59.1 1.7 %collective-permute-start = (f32[4,1,128,128]{3,2,1,0:T(8,128)S(1)}, f32[4,1,128,128]{3,2,1,0:T(8,128)S(1)}, u32[]{:S(2)}, u32[]{:S(2)}) collective-permute-start(f32[4,1,128,128]{3,2,1,0:T(8,128)S(1)} %pad_maximum_fusion), channel_id=1, source_target_pairs={{0,32},{32,0},{64,96},{96,64},{128,160},{160,128},{192,224},{224,1... | collective-permute-start | bytes 786440 | tf_op jit(solution)/shard_map/ppermute | solution.py:11
  62.2 4.8 %collective-permute-done = f32[4,1,128,128]{3,2,1,0:T(8,128)S(1)} collective-permute-done((f32[4,1,128,128]{3,2,1,0:T(8,128)S(1)}, f32[4,1,128,128]{3,2,1,0:T(8,128)S(1)}, u32[]{:S(2)}, u32[]{:S(2)}) %collective-permute-start) | collective-permute-done | bytes 262176 | tf_op jit(solution)/shard_map/ppermute | solution.py:11
  67.1 3.1 %collective-permute-start.1 = (f32[3,1,128,128]{3,2,1,0:T(8,128)S(1)}, f32[3,1,128,128]{3,2,1,0:T(8,128)S(1)}, u32[]{:S(2)}, u32[]{:S(2)}) collective-permute-start(f32[3,1,128,128]{3,2,1,0:T(8,128)S(1)} %pad_maximum_fusion.1), channel_id=1, source_target_pairs={{0,64},{32,96},{64,0},{96,32},{128,192},{160,224},{192,128},{224,1... | collective-permute-start | bytes 589832 | tf_op jit(solution)/shard_map/ppermute | solution.py:11
  70.2 8.6 %collective-permute-done.1 = f32[3,1,128,128]{3,2,1,0:T(8,128)S(1)} collective-permute-done((f32[3,1,128,128]{3,2,1,0:T(8,128)S(1)}, f32[3,1,128,128]{3,2,1,0:T(8,128)S(1)}, u32[]{:S(2)}, u32[]{:S(2)}) %collective-permute-start.1) | collective-permute-done | bytes 196640 | tf_op jit(solution)/shard_map/ppermute | solution.py:11
  78.8 6.5 %collective-permute-start.2 = (f32[2,1,128,128]{3,2,1,0:T(8,128)S(1)}, f32[2,1,128,128]{3,2,1,0:T(8,128)S(1)}, u32[]{:S(2)}, u32[]{:S(2)}) collective-permute-start(f32[2,1,128,128]{3,2,1,0:T(8,128)S(1)} %pad_maximum_fusion.2), channel_id=1, source_target_pairs={{0,128},{32,160},{64,192},{96,224},{128,0},{160,32},{192,64},{224,... | collective-permute-start | bytes 393224 | tf_op jit(solution)/shard_map/ppermute | solution.py:11
  85.3 2.9 %collective-permute-done.2 = f32[2,1,128,128]{3,2,1,0:T(8,128)S(1)} collective-permute-done((f32[2,1,128,128]{3,2,1,0:T(8,128)S(1)}, f32[2,1,128,128]{3,2,1,0:T(8,128)S(1)}, u32[]{:S(2)}, u32[]{:S(2)}) %collective-permute-start.2) | collective-permute-done | bytes 131104 | tf_op jit(solution)/shard_map/ppermute | solution.py:11
  90.3 7.9 %all-to-all-start.6 = ((bf16[32,2,1024]{2,1,0:T(2,128)(2,1)}), bf16[32,2,1024]{2,1,0:T(2,128)(2,1)S(1)}, u32[]{:S(2)}, u32[]{:S(2)}) async-start(bf16[32,2,1024]{2,1,0:T(2,128)(2,1)} %reshape.490), calls=%async_computation.6 | async-start | bytes 262144 | tf_op jit(solution)/shard_map/all_to_all | solution.py:155
  102.0 4.0 %all-to-all-done.6 = bf16[32,2,1024]{2,1,0:T(2,128)(2,1)S(1)} async-done(((bf16[32,2,1024]{2,1,0:T(2,128)(2,1)}), bf16[32,2,1024]{2,1,0:T(2,128)(2,1)S(1)}, u32[]{:S(2)}, u32[]{:S(2)}) %all-to-all-start.6) | async-done | bytes 131104 | tf_op jit(solution)/shard_map/all_to_all | solution.py:155
  105.9 3.9 %all-to-all-start.5 = ((bf16[32,2,1024]{2,1,0:T(2,128)(2,1)}), bf16[32,2,1024]{2,1,0:T(2,128)(2,1)S(1)}, u32[]{:S(2)}, u32[]{:S(2)}) async-start(bf16[32,2,1024]{2,1,0:T(2,128)(2,1)} %reshape.488), calls=%async_computation.5 | async-start | bytes 262144 | tf_op jit(solution)/shard_map/all_to_all | solution.py:152
  110.6 7.0 %all-to-all-done.5 = bf16[32,2,1024]{2,1,0:T(2,128)(2,1)S(1)} async-done(((bf16[32,2,1024]{2,1,0:T(2,128)(2,1)}), bf16[32,2,1024]{2,1,0:T(2,128)(2,1)S(1)}, u32[]{:S(2)}, u32[]{:S(2)}) %all-to-all-start.5) | async-done | bytes 131104 | tf_op jit(solution)/shard_map/all_to_all | solution.py:152
  117.6 3.9 %all-to-all-start.4 = ((bf16[32,2,1024]{2,1,0:T(2,128)(2,1)}), bf16[32,2,1024]{2,1,0:T(2,128)(2,1)S(1)}, u32[]{:S(2)}, u32[]{:S(2)}) async-start(bf16[32,2,1024]{2,1,0:T(2,128)(2,1)} %reshape.486), calls=%async_computation.4 | async-start | bytes 262144 | tf_op jit(solution)/shard_map/all_to_all | solution.py:149
  123.9 5.3 %all-to-all-done.4 = bf16[32,2,1024]{2,1,0:T(2,128)(2,1)S(1)} async-done(((bf16[32,2,1024]{2,1,0:T(2,128)(2,1)}), bf16[32,2,1024]{2,1,0:T(2,128)(2,1)S(1)}, u32[]{:S(2)}, u32[]{:S(2)}) %all-to-all-start.4) | async-done | bytes 131104 | tf_op jit(solution)/shard_map/all_to_all | solution.py:149
  (70 shorter events, 14.3 us)
Async XLA Ops:
  2.2 8.7 %copy-start = (bf16[16,32,128]{2,1,0:T(8,128)(2,1)S(1)}, bf16[16,32,128]{2,1,0:T(8,128)(2,1)}, u32[]{:S(2)}) copy-start(bf16[16,32,128]{2,1,0:T(8,128)(2,1)} %param.8) | copy-start | bytes 393220
  2.2 16.3 %all-to-all-start = ((bf16[16,32,128]{2,0,1:T(8,128)(2,1)}), bf16[16,32,128]{2,0,1:T(8,128)(2,1)S(1)}, u32[]{:S(2)}, u32[]{:S(2)}) async-start(bf16[16,32,128]{2,0,1:T(8,128)(2,1)} %copy.54), calls=%async_computation | async-start | bytes 262144 | tf_op jit(solution)/shard_map/all_to_all | solution.py:113
  11.7 10.8 %copy-start.1 = (bf16[16,32,128]{2,1,0:T(8,128)(2,1)S(1)}, bf16[16,32,128]{2,1,0:T(8,128)(2,1)}, u32[]{:S(2)}) copy-start(bf16[16,32,128]{2,1,0:T(8,128)(2,1)} %param.7) | copy-start | bytes 393220
  18.6 11.6 %all-to-all-start.1 = ((bf16[16,32,128]{2,0,1:T(8,128)(2,1)}), bf16[16,32,128]{2,0,1:T(8,128)(2,1)S(1)}, u32[]{:S(2)}, u32[]{:S(2)}) async-start(bf16[16,32,128]{2,0,1:T(8,128)(2,1)} %copy.55), calls=%async_computation.1 | async-start | bytes 262144 | tf_op jit(solution)/shard_map/all_to_all | solution.py:112
  23.2 10.9 %copy-start.3 = (f32[1,13,512]{2,0,1:T(1,128)S(1)}, f32[1,13,512]{2,0,1:T(1,128)}, u32[]{:S(2)}) copy-start(f32[1,13,512]{2,0,1:T(1,128)} %param.10) | copy-start | bytes 79876
  30.2 11.6 %all-to-all-start.2 = ((bf16[16,32,128]{2,0,1:T(8,128)(2,1)}), bf16[16,32,128]{2,0,1:T(8,128)(2,1)S(1)}, u32[]{:S(2)}, u32[]{:S(2)}) async-start(bf16[16,32,128]{2,0,1:T(8,128)(2,1)} %copy.58), calls=%async_computation.2 | async-start | bytes 262144 | tf_op jit(solution)/shard_map/all_to_all | solution.py:111
  34.1 0.9 copy-start.2
  41.8 11.6 %all-to-all-start.3 = ((bf16[16,32,128]{2,0,1:T(8,128)(2,1)}), bf16[16,32,128]{2,0,1:T(8,128)(2,1)S(1)}, u32[]{:S(2)}, u32[]{:S(2)}) async-start(bf16[16,32,128]{2,0,1:T(8,128)(2,1)} %copy.62), calls=%async_computation.3 | async-start | bytes 262144 | tf_op jit(solution)/shard_map/all_to_all | solution.py:110
  58.5 2.3 %copy-start.5 = (f32[512,512]{0,1:T(8,128)S(1)}, f32[512,512]{0,1:T(8,128)}, u32[]{:S(2)}) copy-start(f32[512,512]{0,1:T(8,128)} %get-tuple-element.48) | copy-start | bytes 3145732
  59.1 7.9 %collective-permute-start = (f32[4,1,128,128]{3,2,1,0:T(8,128)S(1)}, f32[4,1,128,128]{3,2,1,0:T(8,128)S(1)}, u32[]{:S(2)}, u32[]{:S(2)}) collective-permute-start(f32[4,1,128,128]{3,2,1,0:T(8,128)S(1)} %pad_maximum_fusion), channel_id=1, source_target_pairs={{0,32},{32,0},{64,96},{96,64},{128,160},{160,128},{192,224},{224,1... | collective-permute-start | bytes 786440 | tf_op jit(solution)/shard_map/ppermute | solution.py:11
  67.1 11.7 %collective-permute-start.1 = (f32[3,1,128,128]{3,2,1,0:T(8,128)S(1)}, f32[3,1,128,128]{3,2,1,0:T(8,128)S(1)}, u32[]{:S(2)}, u32[]{:S(2)}) collective-permute-start(f32[3,1,128,128]{3,2,1,0:T(8,128)S(1)} %pad_maximum_fusion.1), channel_id=1, source_target_pairs={{0,64},{32,96},{64,0},{96,32},{128,192},{160,224},{192,128},{224,1... | collective-permute-start | bytes 589832 | tf_op jit(solution)/shard_map/ppermute | solution.py:11
  78.8 9.5 %collective-permute-start.2 = (f32[2,1,128,128]{3,2,1,0:T(8,128)S(1)}, f32[2,1,128,128]{3,2,1,0:T(8,128)S(1)}, u32[]{:S(2)}, u32[]{:S(2)}) collective-permute-start(f32[2,1,128,128]{3,2,1,0:T(8,128)S(1)} %pad_maximum_fusion.2), channel_id=1, source_target_pairs={{0,128},{32,160},{64,192},{96,224},{128,0},{160,32},{192,64},{224,... | collective-permute-start | bytes 393224 | tf_op jit(solution)/shard_map/ppermute | solution.py:11
  90.3 15.6 %all-to-all-start.6 = ((bf16[32,2,1024]{2,1,0:T(2,128)(2,1)}), bf16[32,2,1024]{2,1,0:T(2,128)(2,1)S(1)}, u32[]{:S(2)}, u32[]{:S(2)}) async-start(bf16[32,2,1024]{2,1,0:T(2,128)(2,1)} %reshape.490), calls=%async_computation.6 | async-start | bytes 262144 | tf_op jit(solution)/shard_map/all_to_all | solution.py:155
  105.9 11.6 %all-to-all-start.5 = ((bf16[32,2,1024]{2,1,0:T(2,128)(2,1)}), bf16[32,2,1024]{2,1,0:T(2,128)(2,1)S(1)}, u32[]{:S(2)}, u32[]{:S(2)}) async-start(bf16[32,2,1024]{2,1,0:T(2,128)(2,1)} %reshape.488), calls=%async_computation.5 | async-start | bytes 262144 | tf_op jit(solution)/shard_map/all_to_all | solution.py:152
  109.9 0.7 copy-start.4
  117.6 11.6 %all-to-all-start.4 = ((bf16[32,2,1024]{2,1,0:T(2,128)(2,1)}), bf16[32,2,1024]{2,1,0:T(2,128)(2,1)S(1)}, u32[]{:S(2)}, u32[]{:S(2)}) async-start(bf16[32,2,1024]{2,1,0:T(2,128)(2,1)} %reshape.486), calls=%async_computation.4 | async-start | bytes 262144 | tf_op jit(solution)/shard_map/all_to_all | solution.py:149
where the time goes:
time: 131 us; the launch traced here: 130 us
  waiting for transfers between devices  59.8 us (46%)
  starting transfers between devices  47.6 us (36%)
  local copies, waits for them, and re-layouts  11.5 us (9%)
  other arithmetic  5.47 us (4%)
  matrix products  4.65 us (4%)
    ppermute x3, waiting for transfers between devices, partner(): return lax.ppermute(value, axis, pairs)  16.3 us
    ppermute x3, starting transfers between devices, partner(): return lax.ppermute(value, axis, pairs)  11.4 us
    unnamed x29, local copies, waits for them, and re-layouts  10.4 us
    all_to_all x1, starting transfers between devices, on_device(): lax.all_to_all(out_grad, 'head', split_axis=1, concat_axis=0, tiled=True)  8.71 us
    all_to_all x1, starting transfers between devices, on_device(): lax.all_to_all(value_total.astype(jnp.bfloat16), 'head', split_axis=0, co...  7.89 us
    all_to_all x1, waiting for transfers between devices, on_device(): lax.all_to_all(queries, 'head', split_axis=1, concat_axis=0, tiled=True)  7.31 us
    all_to_all x1, waiting for transfers between devices, on_device(): lax.all_to_all(values, 'head', split_axis=1, concat_axis=0, tiled=True)  6.99 us
    all_to_all x1, waiting for transfers between devices, on_device(): lax.all_to_all(key_total.astype(jnp.bfloat16), 'head', split_axis=0, conc...  6.98 us
  transfers between devices with their start and end apart: 10, of which 10 were waited for; matrix products, arithmetic and copies ran while one was open for 8% of the time, Pallas kernels for 0%

commit v1 on v0

--- a/solution.py
+++ b/solution.py
@@ -152,8 +152,16 @@
         lax.all_to_all(
             key_total.astype(jnp.bfloat16), "head", split_axis=0, concat_axis=1, tiled=True
         ),
-        lax.all_to_all(
-            value_total.astype(jnp.bfloat16), "head", split_axis=0, concat_axis=1, tiled=True
+        jnp.concatenate(
+            lax.all_to_all(
+                jnp.stack(
+                    jnp.split(value_total.astype(jnp.bfloat16), lax.axis_size("head"), axis=0)
+                ),
+                "head",
+                0,
+                0,
+            ),
+            axis=1,
         ),
     )
     return (query_out, key_out, value_out, weight_grad)

time: 131 us -> 148 us (1.13)
  local copies, waits for them, and re-layouts: 11.5 us -> 29.7 us
    unnamed x29 -> x57, local copies, waits for them, and re-layouts: 10.4 us -> 27.9 us
  transfers between devices with their start and end apart: 10 -> 10, of which waited for: 10 -> 10; matrix products, arithmetic and copies ran while one was open for 8% -> 7% of each run, Pallas kernels for 0% -> 0%
where the time goes in v1:
time: 148 us; the launch traced here: 147 us
  waiting for transfers between devices  59.3 us (40%)
  starting transfers between devices  47.7 us (32%)
  local copies, waits for them, and re-layouts  29.7 us (20%)
  other arithmetic  4.8 us (3%)
  matrix products  4.65 us (3%)
    unnamed x57, local copies, waits for them, and re-layouts  27.9 us
    ppermute x3, waiting for transfers between devices, partner(): return lax.ppermute(value, axis, pairs)  16.3 us
    ppermute x3, starting transfers between devices, partner(): return lax.ppermute(value, axis, pairs)  11.4 us
    all_to_all x1, starting transfers between devices, on_device(): lax.all_to_all(out_grad, 'head', split_axis=1, concat_axis=0, tiled=True)  8.71 us
    all_to_all x1, starting transfers between devices, on_device(): lax.all_to_all(jnp.stack(jnp.split(value_total.astype(jnp.bfloat16), lax....  7.89 us
    all_to_all x1, waiting for transfers between devices, on_device(): lax.all_to_all(queries, 'head', split_axis=1, concat_axis=0, tiled=True)  7.31 us
    all_to_all x1, waiting for transfers between devices, on_device(): lax.all_to_all(values, 'head', split_axis=1, concat_axis=0, tiled=True)  6.99 us
    all_to_all x1, waiting for transfers between devices, on_device(): lax.all_to_all(out_grad, 'head', split_axis=1, concat_axis=0, tiled=True)  6.88 us
  transfers between devices with their start and end apart: 10, of which 10 were waited for; matrix products, arithmetic and copies ran while one was open for 7% of the time, Pallas kernels for 0%

profile of v1, /device:TPU:1, one launch (start us, length us, event | category | flops | bytes accessed | tf_op | source)
XLA Modules:
  0.0 147.2 jit_solution(2801957886462717193)
XLA Ops:
  0.6 1.6 %copy.53 = bf16[16,32,128]{2,0,1:T(8,128)(2,1)} copy(bf16[16,32,128]{2,1,0:T(8,128)(2,1)} %param.9) | data formatting | bytes 262144 | tf_op args[3]
  2.2 8.7 %all-to-all-start = ((bf16[16,32,128]{2,0,1:T(8,128)(2,1)}), bf16[16,32,128]{2,0,1:T(8,128)(2,1)S(1)}, u32[]{:S(2)}, u32[]{:S(2)}) async-start(bf16[16,32,128]{2,0,1:T(8,128)(2,1)} %copy.53), calls=%async_computation | async-start | bytes 262144 | tf_op jit(solution)/shard_map/all_to_all | solution.py:113
  11.7 6.9 %all-to-all-done = bf16[16,32,128]{2,0,1:T(8,128)(2,1)S(1)} async-done(((bf16[16,32,128]{2,0,1:T(8,128)(2,1)}), bf16[16,32,128]{2,0,1:T(8,128)(2,1)S(1)}, u32[]{:S(2)}, u32[]{:S(2)}) %all-to-all-start) | async-done | bytes 131104 | tf_op jit(solution)/shard_map/all_to_all | solution.py:113
  18.6 3.9 %all-to-all-start.1 = ((bf16[16,32,128]{2,0,1:T(8,128)(2,1)}), bf16[16,32,128]{2,0,1:T(8,128)(2,1)S(1)}, u32[]{:S(2)}, u32[]{:S(2)}) async-start(bf16[16,32,128]{2,0,1:T(8,128)(2,1)} %copy.54), calls=%async_computation.1 | async-start | bytes 262144 | tf_op jit(solution)/shard_map/all_to_all | solution.py:112
  23.2 7.0 %all-to-all-done.1 = bf16[16,32,128]{2,0,1:T(8,128)(2,1)S(1)} async-done(((bf16[16,32,128]{2,0,1:T(8,128)(2,1)}), bf16[16,32,128]{2,0,1:T(8,128)(2,1)S(1)}, u32[]{:S(2)}, u32[]{:S(2)}) %all-to-all-start.1) | async-done | bytes 131104 | tf_op jit(solution)/shard_map/all_to_all | solution.py:112
  30.2 3.9 %all-to-all-start.2 = ((bf16[16,32,128]{2,0,1:T(8,128)(2,1)}), bf16[16,32,128]{2,0,1:T(8,128)(2,1)S(1)}, u32[]{:S(2)}, u32[]{:S(2)}) async-start(bf16[16,32,128]{2,0,1:T(8,128)(2,1)} %copy.57), calls=%async_computation.2 | async-start | bytes 262144 | tf_op jit(solution)/shard_map/all_to_all | solution.py:111
  34.2 0.8 copy-done.2
  35.9 6.0 %all-to-all-done.2 = bf16[16,32,128]{2,0,1:T(8,128)(2,1)S(1)} async-done(((bf16[16,32,128]{2,0,1:T(8,128)(2,1)}), bf16[16,32,128]{2,0,1:T(8,128)(2,1)S(1)}, u32[]{:S(2)}, u32[]{:S(2)}) %all-to-all-start.2) | async-done | bytes 131104 | tf_op jit(solution)/shard_map/all_to_all | solution.py:111
  41.8 3.9 %all-to-all-start.3 = ((bf16[16,32,128]{2,0,1:T(8,128)(2,1)}), bf16[16,32,128]{2,0,1:T(8,128)(2,1)S(1)}, u32[]{:S(2)}, u32[]{:S(2)}) async-start(bf16[16,32,128]{2,0,1:T(8,128)(2,1)} %copy.61), calls=%async_computation.3 | async-start | bytes 262144 | tf_op jit(solution)/shard_map/all_to_all | solution.py:110
  46.2 7.3 %all-to-all-done.3 = bf16[16,32,128]{2,0,1:T(8,128)(2,1)S(1)} async-done(((bf16[16,32,128]{2,0,1:T(8,128)(2,1)}), bf16[16,32,128]{2,0,1:T(8,128)(2,1)S(1)}, u32[]{:S(2)}, u32[]{:S(2)}) %all-to-all-start.3) | async-done | bytes 131104 | tf_op jit(solution)/shard_map/all_to_all | solution.py:110
  53.5 1.7 %fusion.9 = (f32[512,512]{0,1:T(8,128)S(1)}, bf16[512,512]{0,1:T(8,128)(2,1)S(1)}, f32[512,512]{0,1:T(8,128)}) fusion(f32[512,512]{0,1:T(8,128)S(1)} %fusion.61, f32[512]{0:T(512)S(1)} %bitcast.310, f32[512]{0:T(512)S(1)} %bitcast.312, f32[512]{0:T(512)S(1)} %bitcast.314, f32[512]{0:T(512)S(1)} %bitcast.316, f32[512]{0:T(512)S(1)} %bitcast.318, ...), kind=kOutput, calls=%fused_computation.11 | convolution fusion | flops 83361792 | bytes 3952640 | tf_op jit(solution)/shard_map/thd,shd->hts/dot_general | solution.py:82
  55.2 3.1 %select_reduce_fusion = (f32[512]{0:T(512)S(1)}, f32[512]{0:T(512)S(1)}, f32[512]{0:T(512)S(1)}, f32[512]{0:T(512)S(1)}, f32[512]{0:T(512)S(1)}, /*index=5*/f32[...) fusion(f32[512,512]{0,1:T(8,128)S(1)} %get-tuple-element.32), kind=kLoop, calls=%fused_computation.35 | loop fusion | flops 17820672 | bytes 1069056 | tf_op jit(solution)/shard_map/reduce_sum | solution.py:91
  59.1 1.7 %collective-permute-start = (f32[4,1,128,128]{3,2,1,0:T(8,128)S(1)}, f32[4,1,128,128]{3,2,1,0:T(8,128)S(1)}, u32[]{:S(2)}, u32[]{:S(2)}) collective-permute-start(f32[4,1,128,128]{3,2,1,0:T(8,128)S(1)} %pad_maximum_fusion), channel_id=1, source_target_pairs={{0,32},{32,0},{64,96},{96,64},{128,160},{160,128},{192,224},{224,1... | collective-permute-start | bytes 786440 | tf_op jit(solution)/shard_map/ppermute | solution.py:11
  62.2 4.8 %collective-permute-done = f32[4,1,128,128]{3,2,1,0:T(8,128)S(1)} collective-permute-done((f32[4,1,128,128]{3,2,1,0:T(8,128)S(1)}, f32[4,1,128,128]{3,2,1,0:T(8,128)S(1)}, u32[]{:S(2)}, u32[]{:S(2)}) %collective-permute-start) | collective-permute-done | bytes 262176 | tf_op jit(solution)/shard_map/ppermute | solution.py:11
  67.1 3.1 %collective-permute-start.1 = (f32[3,1,128,128]{3,2,1,0:T(8,128)S(1)}, f32[3,1,128,128]{3,2,1,0:T(8,128)S(1)}, u32[]{:S(2)}, u32[]{:S(2)}) collective-permute-start(f32[3,1,128,128]{3,2,1,0:T(8,128)S(1)} %pad_maximum_fusion.1), channel_id=1, source_target_pairs={{0,64},{32,96},{64,0},{96,32},{128,192},{160,224},{192,128},{224,1... | collective-permute-start | bytes 589832 | tf_op jit(solution)/shard_map/ppermute | solution.py:11
  70.2 8.6 %collective-permute-done.1 = f32[3,1,128,128]{3,2,1,0:T(8,128)S(1)} collective-permute-done((f32[3,1,128,128]{3,2,1,0:T(8,128)S(1)}, f32[3,1,128,128]{3,2,1,0:T(8,128)S(1)}, u32[]{:S(2)}, u32[]{:S(2)}) %collective-permute-start.1) | collective-permute-done | bytes 196640 | tf_op jit(solution)/shard_map/ppermute | solution.py:11
  78.8 6.5 %collective-permute-start.2 = (f32[2,1,128,128]{3,2,1,0:T(8,128)S(1)}, f32[2,1,128,128]{3,2,1,0:T(8,128)S(1)}, u32[]{:S(2)}, u32[]{:S(2)}) collective-permute-start(f32[2,1,128,128]{3,2,1,0:T(8,128)S(1)} %pad_maximum_fusion.2), channel_id=1, source_target_pairs={{0,128},{32,160},{64,192},{96,224},{128,0},{160,32},{192,64},{224,... | collective-permute-start | bytes 393224 | tf_op jit(solution)/shard_map/ppermute | solution.py:11
  85.3 2.9 %collective-permute-done.2 = f32[2,1,128,128]{3,2,1,0:T(8,128)S(1)} collective-permute-done((f32[2,1,128,128]{3,2,1,0:T(8,128)S(1)}, f32[2,1,128,128]{3,2,1,0:T(8,128)S(1)}, u32[]{:S(2)}, u32[]{:S(2)}) %collective-permute-start.2) | collective-permute-done | bytes 131104 | tf_op jit(solution)/shard_map/ppermute | solution.py:11
  107.5 7.9 %all-to-all-start.6 = ((bf16[32,16,1,128]{3,1,2,0:T(8,128)(2,1)}), bf16[32,16,1,128]{3,1,2,0:T(8,128)(2,1)S(1)}, u32[]{:S(2)}, u32[]{:S(2)}) async-start(bf16[32,16,1,128]{3,1,2,0:T(8,128)(2,1)} %constant_dynamic-update-slice_fusion), calls=%async_computation.6 | async-start | bytes 262144 | tf_op jit(solution)/shard_map/all_to_all | solution.py:156
  119.6 3.5 %all-to-all-done.6 = bf16[32,16,1,128]{3,1,2,0:T(8,128)(2,1)S(1)} async-done(((bf16[32,16,1,128]{3,1,2,0:T(8,128)(2,1)}), bf16[32,16,1,128]{3,1,2,0:T(8,128)(2,1)S(1)}, u32[]{:S(2)}, u32[]{:S(2)}) %all-to-all-start.6) | async-done | bytes 131104 | tf_op jit(solution)/shard_map/all_to_all | solution.py:156
  123.1 4.0 %all-to-all-start.5 = ((bf16[32,2,1024]{2,1,0:T(2,128)(2,1)}), bf16[32,2,1024]{2,1,0:T(2,128)(2,1)S(1)}, u32[]{:S(2)}, u32[]{:S(2)}) async-start(bf16[32,2,1024]{2,1,0:T(2,128)(2,1)} %reshape.496), calls=%async_computation.5 | async-start | bytes 262144 | tf_op jit(solution)/shard_map/all_to_all | solution.py:152
  127.8 6.9 %all-to-all-done.5 = bf16[32,2,1024]{2,1,0:T(2,128)(2,1)S(1)} async-done(((bf16[32,2,1024]{2,1,0:T(2,128)(2,1)}), bf16[32,2,1024]{2,1,0:T(2,128)(2,1)S(1)}, u32[]{:S(2)}, u32[]{:S(2)}) %all-to-all-start.5) | async-done | bytes 131104 | tf_op jit(solution)/shard_map/all_to_all | solution.py:152
  134.7 3.9 %all-to-all-start.4 = ((bf16[32,2,1024]{2,1,0:T(2,128)(2,1)}), bf16[32,2,1024]{2,1,0:T(2,128)(2,1)S(1)}, u32[]{:S(2)}, u32[]{:S(2)}) async-start(bf16[32,2,1024]{2,1,0:T(2,128)(2,1)} %reshape.494), calls=%async_computation.4 | async-start | bytes 262144 | tf_op jit(solution)/shard_map/all_to_all | solution.py:149
  140.9 5.5 %all-to-all-done.4 = bf16[32,2,1024]{2,1,0:T(2,128)(2,1)S(1)} async-done(((bf16[32,2,1024]{2,1,0:T(2,128)(2,1)}), bf16[32,2,1024]{2,1,0:T(2,128)(2,1)S(1)}, u32[]{:S(2)}, u32[]{:S(2)}) %all-to-all-start.4) | async-done | bytes 131104 | tf_op jit(solution)/shard_map/all_to_all | solution.py:149
  (98 shorter events, 31.9 us)
Async XLA Ops:
  2.2 8.7 %copy-start = (bf16[16,32,128]{2,1,0:T(8,128)(2,1)S(1)}, bf16[16,32,128]{2,1,0:T(8,128)(2,1)}, u32[]{:S(2)}) copy-start(bf16[16,32,128]{2,1,0:T(8,128)(2,1)} %param.8) | copy-start | bytes 393220
  2.2 16.3 %all-to-all-start = ((bf16[16,32,128]{2,0,1:T(8,128)(2,1)}), bf16[16,32,128]{2,0,1:T(8,128)(2,1)S(1)}, u32[]{:S(2)}, u32[]{:S(2)}) async-start(bf16[16,32,128]{2,0,1:T(8,128)(2,1)} %copy.53), calls=%async_computation | async-start | bytes 262144 | tf_op jit(solution)/shard_map/all_to_all | solution.py:113
  11.7 10.8 %copy-start.1 = (bf16[16,32,128]{2,1,0:T(8,128)(2,1)S(1)}, bf16[16,32,128]{2,1,0:T(8,128)(2,1)}, u32[]{:S(2)}) copy-start(bf16[16,32,128]{2,1,0:T(8,128)(2,1)} %param.7) | copy-start | bytes 393220
  18.6 11.6 %all-to-all-start.1 = ((bf16[16,32,128]{2,0,1:T(8,128)(2,1)}), bf16[16,32,128]{2,0,1:T(8,128)(2,1)S(1)}, u32[]{:S(2)}, u32[]{:S(2)}) async-start(bf16[16,32,128]{2,0,1:T(8,128)(2,1)} %copy.54), calls=%async_computation.1 | async-start | bytes 262144 | tf_op jit(solution)/shard_map/all_to_all | solution.py:112
  23.2 10.9 %copy-start.3 = (f32[1,13,512]{2,0,1:T(1,128)S(1)}, f32[1,13,512]{2,0,1:T(1,128)}, u32[]{:S(2)}) copy-start(f32[1,13,512]{2,0,1:T(1,128)} %param.10) | copy-start | bytes 79876
  30.2 11.6 %all-to-all-start.2 = ((bf16[16,32,128]{2,0,1:T(8,128)(2,1)}), bf16[16,32,128]{2,0,1:T(8,128)(2,1)S(1)}, u32[]{:S(2)}, u32[]{:S(2)}) async-start(bf16[16,32,128]{2,0,1:T(8,128)(2,1)} %copy.57), calls=%async_computation.2 | async-start | bytes 262144 | tf_op jit(solution)/shard_map/all_to_all | solution.py:111
  34.1 0.9 copy-start.2
  41.8 11.6 %all-to-all-start.3 = ((bf16[16,32,128]{2,0,1:T(8,128)(2,1)}), bf16[16,32,128]{2,0,1:T(8,128)(2,1)S(1)}, u32[]{:S(2)}, u32[]{:S(2)}) async-start(bf16[16,32,128]{2,0,1:T(8,128)(2,1)} %copy.61), calls=%async_computation.3 | async-start | bytes 262144 | tf_op jit(solution)/shard_map/all_to_all | solution.py:110
  58.5 2.3 %copy-start.5 = (f32[512,512]{0,1:T(8,128)S(1)}, f32[512,512]{0,1:T(8,128)}, u32[]{:S(2)}) copy-start(f32[512,512]{0,1:T(8,128)} %get-tuple-element.52) | copy-start | bytes 3145732
  59.1 7.9 %collective-permute-start = (f32[4,1,128,128]{3,2,1,0:T(8,128)S(1)}, f32[4,1,128,128]{3,2,1,0:T(8,128)S(1)}, u32[]{:S(2)}, u32[]{:S(2)}) collective-permute-start(f32[4,1,128,128]{3,2,1,0:T(8,128)S(1)} %pad_maximum_fusion), channel_id=1, source_target_pairs={{0,32},{32,0},{64,96},{96,64},{128,160},{160,128},{192,224},{224,1... | collective-permute-start | bytes 786440 | tf_op jit(solution)/shard_map/ppermute | solution.py:11
  67.1 11.7 %collective-permute-start.1 = (f32[3,1,128,128]{3,2,1,0:T(8,128)S(1)}, f32[3,1,128,128]{3,2,1,0:T(8,128)S(1)}, u32[]{:S(2)}, u32[]{:S(2)}) collective-permute-start(f32[3,1,128,128]{3,2,1,0:T(8,128)S(1)} %pad_maximum_fusion.1), channel_id=1, source_target_pairs={{0,64},{32,96},{64,0},{96,32},{128,192},{160,224},{192,128},{224,1... | collective-permute-start | bytes 589832 | tf_op jit(solution)/shard_map/ppermute | solution.py:11
  78.8 9.5 %collective-permute-start.2 = (f32[2,1,128,128]{3,2,1,0:T(8,128)S(1)}, f32[2,1,128,128]{3,2,1,0:T(8,128)S(1)}, u32[]{:S(2)}, u32[]{:S(2)}) collective-permute-start(f32[2,1,128,128]{3,2,1,0:T(8,128)S(1)} %pad_maximum_fusion.2), channel_id=1, source_target_pairs={{0,128},{32,160},{64,192},{96,224},{128,0},{160,32},{192,64},{224,... | collective-permute-start | bytes 393224 | tf_op jit(solution)/shard_map/ppermute | solution.py:11
  107.5 15.6 %all-to-all-start.6 = ((bf16[32,16,1,128]{3,1,2,0:T(8,128)(2,1)}), bf16[32,16,1,128]{3,1,2,0:T(8,128)(2,1)S(1)}, u32[]{:S(2)}, u32[]{:S(2)}) async-start(bf16[32,16,1,128]{3,1,2,0:T(8,128)(2,1)} %constant_dynamic-update-slice_fusion), calls=%async_computation.6 | async-start | bytes 262144 | tf_op jit(solution)/shard_map/all_to_all | solution.py:156
  123.1 11.6 %all-to-all-start.5 = ((bf16[32,2,1024]{2,1,0:T(2,128)(2,1)}), bf16[32,2,1024]{2,1,0:T(2,128)(2,1)S(1)}, u32[]{:S(2)}, u32[]{:S(2)}) async-start(bf16[32,2,1024]{2,1,0:T(2,128)(2,1)} %reshape.496), calls=%async_computation.5 | async-start | bytes 262144 | tf_op jit(solution)/shard_map/all_to_all | solution.py:152
  127.1 0.7 copy-start.4
  134.7 11.6 %all-to-all-start.4 = ((bf16[32,2,1024]{2,1,0:T(2,128)(2,1)}), bf16[32,2,1024]{2,1,0:T(2,128)(2,1)S(1)}, u32[]{:S(2)}, u32[]{:S(2)}) async-start(bf16[32,2,1024]{2,1,0:T(2,128)(2,1)} %reshape.494), calls=%async_computation.4 | async-start | bytes 262144 | tf_op jit(solution)/shard_map/all_to_all | solution.py:149
